TPU v7x, 32 devices: a whole 2x2x4 slice. The times are simulated.
32 devices in a mesh: dp: 16 (over z, y, core), rows: 2 (over x).
Axes of the slice: x: 2, y: 2, z: 4, core: 2. Of those that a mesh axis runs over, the one named last changes fastest.
Arguments:
- latents: bfloat16 [16, 4, 128, 320], P('dp', 'rows'), may hold values from -6 to 6
- mean_one: float32 [16, 32], P('dp'), may hold values from -0.5 to 0.5
- rstd_one: float32 [16, 32], P('dp'), may hold values from 0.5 to 2
- gain_one: float32 [320], replicated, may hold values from 0.25 to 1.75
- shift_one: float32 [320], replicated, may hold values from -0.5 to 0.5
- kernel_one: bfloat16 [4, 9, 25600], P(None, None, 'dp'), may hold values from -0.109375 to 0.109375
- bias_one: float32 [320], replicated, may hold values from -3 to 3
- embed_bias: float32 [16, 320], P('dp'), may hold values from -3 to 3
- mean_two: float32 [16, 32], P('dp'), may hold values from -0.5 to 0.5
- rstd_two: float32 [16, 32], P('dp'), may hold values from 0.5 to 2
- gain_two: float32 [320], replicated, may hold values from 0.25 to 1.75
- shift_two: float32 [320], replicated, may hold values from -0.5 to 0.5
- kernel_two: bfloat16 [4, 9, 25600], P(None, None, 'dp'), may hold values from -0.109375 to 0.109375
- bias_two: float32 [320], replicated, may hold values from -3 to 3
Outputs:
- block_out: bfloat16 [16, 4, 128, 320], P('dp', 'rows')
All inputs are finite; a program needn't handle non-finite values.
Results may differ from a plain program's by a relative error of at most 0.0045.
Values may be sent and summed in bfloat16 or wider, within the bound.
No kernel may reach another device: no remote copies, remote signals or barrier semaphores. Data moves between devices by JAX's collectives and lax.ppermute only.
A program may use at most 192 MiB of HBM per device.

v0:
```python
import jax
import jax.numpy as jnp
from jax import lax
from jax.sharding import PartitionSpec as P


def padded_2(array, sides, width):
    for axis, dim in sides:
        devices, length = (lax.axis_size(axis), array.shape[dim])
        up = [(i, (i + 1) % devices) for i in range(devices - 1)]
        down = [(j, i) for i, j in up]
        last = lax.slice_in_dim(array, length - width, length, axis=dim)
        first = lax.slice_in_dim(array, 0, width, axis=dim)
        before = lax.ppermute(last, axis, up)
        after = lax.ppermute(first, axis, down)
        array = jnp.concatenate([before, array, after], axis=dim)
    return array


def norm_silu(values, group_mean, group_rstd, gain_vec, shift_vec):
    height, columns, channels = values.shape
    groups = group_mean.shape[-1]
    grouped = values.reshape(height, columns, groups, channels // groups)
    scaled = (grouped - group_mean[0][:, None]) * group_rstd[0][:, None]
    return jax.nn.silu(scaled.reshape(height, columns, channels) * gain_vec + shift_vec)


def padded_rows(activation):
    padded = padded_2(activation, (("rows", 0),), 1)
    return jnp.pad(padded, ((0, 0), (1, 1), (0, 0)))


def window_at(padded, position, height, columns, first_channel, depth):
    tap_row = position // 3
    tap_col = position % 3
    window = padded[
        tap_row : tap_row + height,
        tap_col : tap_col + columns,
        first_channel : first_channel + depth,
    ]
    return window.reshape(height * columns, depth)


def reorder_whole(whole_kernel, channels):
    blocks = whole_kernel.shape[0]
    split = whole_kernel.reshape(blocks, 9, channels // blocks, channels)
    return jnp.transpose(split, (1, 0, 2, 3)).reshape(3, 3 * channels, channels)


def whole_weights(kernel, channels):
    whole_kernel = lax.all_gather(kernel, "dp", axis=2, tiled=True)
    return reorder_whole(whole_kernel, channels)


def convolve_whole(activation, weights):
    height, columns, channels = activation.shape
    padded = padded_rows(activation)
    accumulated = jnp.zeros((height * columns, channels), jnp.float32)
    for tap_row in range(3):
        windows = jnp.concatenate(
            [
                window_at(padded, 3 * tap_row + tap_col, height, columns, 0, channels)
                for tap_col in range(3)
            ],
            axis=1,
        )
        accumulated = accumulated + jnp.dot(
            windows, weights[tap_row], preferred_element_type=jnp.float32
        )
    return accumulated.reshape(height, columns, channels)


def shards(
    latents,
    mean_one,
    rstd_one,
    gain_one,
    shift_one,
    kernel_one,
    bias_one,
    embed_bias,
    mean_two,
    rstd_two,
    gain_two,
    shift_two,
    kernel_two,
    bias_two,
):
    channels = latents.shape[3]
    sample = latents[0].astype(jnp.float32)
    first_act = norm_silu(sample, mean_one, rstd_one, gain_one, shift_one).astype(jnp.bfloat16)
    hidden = (
        convolve_whole(first_act, whole_weights(kernel_one, channels)) + bias_one + embed_bias[0]
    )
    second_act = norm_silu(hidden, mean_two, rstd_two, gain_two, shift_two).astype(jnp.bfloat16)
    result = convolve_whole(second_act, whole_weights(kernel_two, channels)) + bias_two + sample
    return result.astype(jnp.bfloat16)[None]


def solution(mesh):
    placed = (
        P("dp", "rows", None, None),
        P("dp", None),
        P("dp", None),
        P(),
        P(),
        P(None, None, "dp"),
        P(),
        P("dp", None),
        P("dp", None),
        P("dp", None),
        P(),
        P(),
        P(None, None, "dp"),
        P(),
    )
    return jax.shard_map(
        shards, mesh=mesh, in_specs=placed, out_specs=P("dp", "rows", None, None), check_vma=False
    )
```

profile of v0, /device:TPU:0, one launch (start us, length us, event | category | flops | bytes accessed | tf_op | source)
XLA Modules:
  0.0 321.2 jit_solution(16401829512371649083)
XLA Ops:
  6.5 3.1 copy.65
  9.8 2.4 copy.77
  12.6 0.3 multiply_convert_fusion.3
  12.9 4.9 %collective-permute-start = (bf16[1,128,320]{1,2,0:T(8,128)(2,1)S(1)}, bf16[1,128,320]{1,2,0:T(8,128)(2,1)S(1)}, u32[]{:S(2)}, u32[]{:S(2)}) collective-permute-start(bf16[1,128,320]{1,2,0:T(8,128)(2,1)S(1)} %get-tuple-element.29), channel_id=1, source_target_pairs={{0,1},{2,3},{4,5},{6,7},{8,9},{10,11},{12,13},{14,15},{16,17},{18,... | collective-permute-start | bytes 245768 | tf_op jit(solution)/shard_map/ppermute | solution.py:14
  17.8 1.3 collective-permute-start.1
  19.1 0.2 copy.68
  19.3 0.9 multiply_convert_fusion.2
  20.4 0.1 sub.49
  20.6 3.5 %collective-permute-done.1 = bf16[1,128,320]{1,2,0:T(8,128)(2,1)S(1)} collective-permute-done((bf16[1,128,320]{1,2,0:T(8,128)(2,1)S(1)}, bf16[1,128,320]{1,2,0:T(8,128)(2,1)S(1)}, u32[]{:S(2)}, u32[]{:S(2)}) %collective-permute-start.1) | collective-permute-done | bytes 81952 | tf_op jit(solution)/shard_map/ppermute | solution.py:15
  24.2 0.3 fusion.5
  24.5 0.2 slice_bitcast_fusion.7
  24.8 0.7 copy_bitcast_fusion.11
  25.5 120.5 %all-gather.3.cloned.1.call-done = bf16[4,9,25600]{1,0,2:T(4,128)(2,1)} async-done(((bf16[4,9,1600]{1,0,2:T(4,128)(2,1)}), bf16[4,9,25600]{1,0,2:T(4,128)(2,1)}) %all-gather.3.cloned.1.call-update) | async-done | bytes 1843216 | tf_op jit(solution)/shard_map/all_gather | solution.py:51
  146.0 30.0 %copy.66 = bf16[4,9,80,320]{3,2,0,1:T(8,128)(2,1)S(1)} copy(bf16[4,9,80,320]{1,0,3,2:T(4,128)(2,1)} %bitcast.136) | data formatting | bytes 3686400 | tf_op jit(solution)/shard_map/reshape | solution.py:46
  176.1 0.2 fusion.62
  176.3 0.4 fusion.6
  176.8 0.4 copy-done.1
  177.3 0.4 convolution_add_fusion.3
  177.8 0.6 multiply_convert_fusion
  178.4 0.3 multiply_convert_fusion.1
  178.8 3.4 %collective-permute-start.2 = (bf16[1,128,320]{1,2,0:T(8,128)(2,1)S(1)}, bf16[1,128,320]{1,2,0:T(8,128)(2,1)S(1)}, u32[]{:S(2)}, u32[]{:S(2)}) collective-permute-start(bf16[1,128,320]{1,2,0:T(8,128)(2,1)S(1)} %get-tuple-element.25), channel_id=1, source_target_pairs={{0,1},{2,3},{4,5},{6,7},{8,9},{10,11},{12,13},{14,15},{16,17},{18,... | collective-permute-start | bytes 245768 | tf_op jit(solution)/shard_map/ppermute | solution.py:14
  182.2 1.3 collective-permute-start.3
  183.5 97.6 %all-gather.5.cloned.1.call-done = bf16[4,9,25600]{1,0,2:T(4,128)(2,1)} async-done(((bf16[4,9,1600]{1,0,2:T(4,128)(2,1)}), bf16[4,9,25600]{1,0,2:T(4,128)(2,1)}) %all-gather.5.cloned.1.call-update) | async-done | bytes 1843216 | tf_op jit(solution)/shard_map/all_gather | solution.py:51
  281.1 29.7 %copy.78 = bf16[4,9,80,320]{3,2,0,1:T(8,128)(2,1)S(1)} copy(bf16[4,9,80,320]{1,0,3,2:T(4,128)(2,1)} %bitcast.135) | data formatting | bytes 3686400 | tf_op jit(solution)/shard_map/reshape | solution.py:46
  310.8 0.2 fusion.61
  311.2 0.3 select_maximum_fusion
  311.5 0.2 slice_bitcast_fusion.1
  312.0 0.4 fusion.22
  312.4 0.4 convolution_add_fusion.1
  312.9 0.4 convolution_add_fusion
  313.3 0.2 reshape.141
  313.5 0.8 fusion.50
  (59 shorter events, 1.4 us)
Async XLA Ops:
  6.5 3.3 %copy-start.3 = (bf16[4,9,1600]{2,0,1:T(4,128)(2,1)S(1)}, bf16[4,9,1600]{2,0,1:T(4,128)(2,1)}, u32[]{:S(2)}) copy-start(bf16[4,9,1600]{2,0,1:T(4,128)(2,1)} %param.26) | copy-start | bytes 345604
  6.5 139.5 %all-gather.3.cloned.1.call-start = ((), (), s32[]{:S(2)}) async-start(), calls=%async_computation | async-start | bytes 27852800 | tf_op jit(solution)/shard_map/all_gather | solution.py:51
  9.7 2.5 copy-start.11
  9.7 2.7 copy-start.12
  9.7 2.9 copy-start
  9.7 2.9 copy-start.4
  9.7 2.9 copy-start.5
  9.7 271.4 %all-gather.5.cloned.1.call-start = ((), (), s32[]{:S(2)}) async-start(), calls=%async_computation.1 | async-start | bytes 27852800 | tf_op jit(solution)/shard_map/all_gather | solution.py:51
  12.2 8.0 %copy-start.13 = (f32[1,32]{1,0:T(1,128)S(1)}, f32[1,32]{1,0:T(1,128)}, u32[]{:S(2)}) copy-start(f32[1,32]{1,0:T(1,128)} %param.23) | copy-start | bytes 388
  12.2 8.2 %copy-start.14 = (f32[1,32]{1,0:T(1,128)S(1)}, f32[1,32]{1,0:T(1,128)}, u32[]{:S(2)}) copy-start(f32[1,32]{1,0:T(1,128)} %param.22) | copy-start | bytes 388
  12.2 8.4 %copy-start.10 = (f32[1,320]{1,0:T(1,128)S(1)}, f32[1,320]{1,0:T(1,128)}, u32[]{:S(2)}) copy-start(f32[1,320]{1,0:T(1,128)} %param.21) | copy-start | bytes 3844
  12.9 7.7 %collective-permute-start = (bf16[1,128,320]{1,2,0:T(8,128)(2,1)S(1)}, bf16[1,128,320]{1,2,0:T(8,128)(2,1)S(1)}, u32[]{:S(2)}, u32[]{:S(2)}) collective-permute-start(bf16[1,128,320]{1,2,0:T(8,128)(2,1)S(1)} %get-tuple-element.29), channel_id=1, source_target_pairs={{0,1},{2,3},{4,5},{6,7},{8,9},{10,11},{12,13},{14,15},{16,17},{18,... | collective-permute-start | bytes 245768 | tf_op jit(solution)/shard_map/ppermute | solution.py:14
  17.8 6.3 %collective-permute-start.1 = (bf16[1,128,320]{1,2,0:T(8,128)(2,1)S(1)}, bf16[1,128,320]{1,2,0:T(8,128)(2,1)S(1)}, u32[]{:S(2)}, u32[]{:S(2)}) collective-permute-start(bf16[1,128,320]{1,2,0:T(8,128)(2,1)S(1)} %get-tuple-element.30), channel_id=1, source_target_pairs={{1,0},{3,2},{5,4},{7,6},{9,8},{11,10},{13,12},{15,14},{17,16},{19,... | collective-permute-start | bytes 245768 | tf_op jit(solution)/shard_map/ppermute | solution.py:15
  176.3 0.9 copy-start.1
  176.3 1.0 copy-start.2
  176.8 1.0 copy-start.6
  176.8 1.0 copy-start.7
  176.8 1.0 copy-start.8
  178.8 132.3 %collective-permute-start.2 = (bf16[1,128,320]{1,2,0:T(8,128)(2,1)S(1)}, bf16[1,128,320]{1,2,0:T(8,128)(2,1)S(1)}, u32[]{:S(2)}, u32[]{:S(2)}) collective-permute-start(bf16[1,128,320]{1,2,0:T(8,128)(2,1)S(1)} %get-tuple-element.25), channel_id=1, source_target_pairs={{0,1},{2,3},{4,5},{6,7},{8,9},{10,11},{12,13},{14,15},{16,17},{18,... | collective-permute-start | bytes 245768 | tf_op jit(solution)/shard_map/ppermute | solution.py:14
  182.2 128.9 %collective-permute-start.3 = (bf16[1,128,320]{1,2,0:T(8,128)(2,1)S(1)}, bf16[1,128,320]{1,2,0:T(8,128)(2,1)S(1)}, u32[]{:S(2)}, u32[]{:S(2)}) collective-permute-start(bf16[1,128,320]{1,2,0:T(8,128)(2,1)S(1)} %get-tuple-element.26), channel_id=1, source_target_pairs={{1,0},{3,2},{5,4},{7,6},{9,8},{11,10},{13,12},{15,14},{17,16},{19,... | collective-permute-start | bytes 245768 | tf_op jit(solution)/shard_map/ppermute | solution.py:15
  312.9 0.7 copy-start.9
Sparse Core Ops, SparseCore 0:
  9.8 136.1 all-gather.2
  147.6 133.4 all-gather.4
where the time goes:
time: 323 us; the launch traced here: 321 us
  waiting for transfers between devices  222 us (69%)
  local copies, waits for them, and re-layouts  68.9 us (21%)
  between operations  13.9 us (4%)
  starting transfers between devices  10.9 us (3%)
    all_gather x2, waiting for transfers between devices, whole_weights(): whole_kernel = lax.all_gather(kernel, 'dp', axis=2, tiled=True)  218 us
    reshape x2, local copies, waits for them, and re-layouts, reorder_whole(): split = whole_kernel.reshape(blocks, 9, channels // blocks, channels)  59.7 us
    ppermute x2, starting transfers between devices, padded_2(): before = lax.ppermute(last, axis, up)  8.29 us
    unnamed x34, local copies, waits for them, and re-layouts  6.57 us
  transfers between devices with their start and end apart: 6, of which 3 were waited for; matrix products, arithmetic and copies ran while one was open for 21% of the time, Pallas kernels for 0%

commit v1 on v0

--- a/solution.py
+++ b/solution.py
@@ -2,6 +2,12 @@
 import jax.numpy as jnp
 from jax import lax
 from jax.sharding import PartitionSpec as P
+
+
+def joined_along(parts, dim):
+    parts = jnp.moveaxis(parts, 0, dim)
+    shape = parts.shape
+    return parts.reshape(*shape[:dim], shape[dim] * shape[dim + 1], *shape[dim + 2 :])
 
 
 def padded_2(array, sides, width):
@@ -48,7 +54,14 @@
 
 
 def whole_weights(kernel, channels):
-    whole_kernel = lax.all_gather(kernel, "dp", axis=2, tiled=True)
+    length_2 = lax.axis_size("dp")
+    right = [(i_2, (i_2 + 1) % length_2) for i_2 in range(length_2)]
+    tiles = [kernel]
+    while len(tiles) < length_2:
+        tiles.append(lax.ppermute(tiles[-1], "dp", right))
+    index = lax.axis_index("dp")
+    tiles = jnp.stack(tiles)[(index - jnp.arange(length_2)) % length_2]
+    whole_kernel = joined_along(tiles, 2)
     return reorder_whole(whole_kernel, channels)
 
 

time: 323 us -> 150 us (0.46)
  waiting for transfers between devices: 222 us -> 75.7 us
  local copies, waits for them, and re-layouts: 68.9 us -> 50.3 us
  between operations: 13.9 us -> 0.56 us
  starting transfers between devices: 10.9 us -> 15.2 us
    all_gather x2 -> x0, waiting for transfers between devices: 218 us -> none  [whole_weights(): whole_kernel = lax.all_gather(kernel, 'dp', axis=2, tiled=True)]
    ppermute x0 -> x30, waiting for transfers between devices: none -> 75.6 us  [whole_weights(): tiles.append(lax.ppermute(tiles[-1], 'dp', right))]
    reshape x2 -> x0, local copies, waits for them, and re-layouts: 59.7 us -> none  [reorder_whole(): split = whole_kernel.reshape(blocks, 9, channels // blocks, channels)]
    unnamed x34 -> x50, local copies, waits for them, and re-layouts: 6.57 us -> 24.5 us
    another operation x0 -> x4, local copies, waits for them, and re-layouts: none -> 10.6 us  [the longest x2 8.31 us: reorder_whole(): split = whole_kernel.reshape(blocks, 9, channels // blocks, channels)]
    gather x0 -> x2, local copies, waits for them, and re-layouts: none -> 7.6 us  [whole_weights(): tiles = jnp.stack(tiles)[(index - jnp.arange(length_2)) % length_2]]
    ppermute x0 -> x30, starting transfers between devices: none -> 3.69 us  [whole_weights(): tiles.append(lax.ppermute(tiles[-1], 'dp', right))]
    ppermute x2, waiting for transfers between devices: 3.53 us -> 0.01 us  [padded_2(): after = lax.ppermute(first, axis, down)]
  transfers between devices with their start and end apart: 6 -> 34, of which waited for: 3 -> 27; matrix products, arithmetic and copies ran while one was open for 21% -> 36% of each run, Pallas kernels for 0% -> 0%
where the time goes in v1:
time: 150 us; the launch traced here: 149 us
  waiting for transfers between devices  75.7 us (50%)
  local copies, waits for them, and re-layouts  50.3 us (34%)
  starting transfers between devices  15.2 us (10%)
  other arithmetic  4.64 us (3%)
  matrix products  2.73 us (2%)
    ppermute x30, waiting for transfers between devices, whole_weights(): tiles.append(lax.ppermute(tiles[-1], 'dp', right))  75.6 us
    unnamed x50, local copies, waits for them, and re-layouts  24.5 us
    ppermute x2, starting transfers between devices, padded_2(): before = lax.ppermute(last, axis, up)  8.67 us
    another operation x2, local copies, waits for them, and re-layouts, reorder_whole(): split = whole_kernel.reshape(blocks, 9, channels // blocks, channels)  8.31 us
    gather x2, local copies, waits for them, and re-layouts, whole_weights(): tiles = jnp.stack(tiles)[(index - jnp.arange(length_2)) % length_2]  7.6 us
    ppermute x30, starting transfers between devices, whole_weights(): tiles.append(lax.ppermute(tiles[-1], 'dp', right))  3.69 us
  transfers between devices with their start and end apart: 34, of which 27 were waited for; matrix products, arithmetic and copies ran while one was open for 36% of the time, Pallas kernels for 0%

profile of v1, /device:TPU:0, one launch (start us, length us, event | category | flops | bytes accessed | tf_op | source)
XLA Modules:
  0.0 149.0 jit_solution(6850089787137108227)
XLA Ops:
  2.2 1.2 multiply_convert_fusion.3
  3.4 4.4 %collective-permute-start = (bf16[1,128,320]{1,2,0:T(8,128)(2,1)S(1)}, bf16[1,128,320]{1,2,0:T(8,128)(2,1)S(1)}, u32[]{:S(2)}, u32[]{:S(2)}) collective-permute-start(bf16[1,128,320]{1,2,0:T(8,128)(2,1)S(1)} %get-tuple-element.29), channel_id=1, source_target_pairs={{0,1},{2,3},{4,5},{6,7},{8,9},{10,11},{12,13},{14,15},{16,17},{18,... | collective-permute-start | bytes 245768 | tf_op jit(solution)/shard_map/ppermute | solution.py:20
  7.9 1.3 collective-permute-start.1
  9.2 1.4 collective-permute-start.19
  10.5 1.6 %bitcast_dynamic-update-slice_fusion.31 = bf16[16,4,9,1600]{3,1,2,0:T(4,128)(2,1)} fusion(bf16[4,9,1600]{2,0,1:T(4,128)(2,1)} %param.19), kind=kLoop, calls=%fused_computation.136 | loop fusion | bytes 235008
  13.2 1.6 %bitcast_dynamic-update-slice_fusion.15 = bf16[16,4,9,1600]{3,1,2,0:T(4,128)(2,1)} fusion(bf16[4,9,1600]{2,0,1:T(4,128)(2,1)} %param.26), kind=kLoop, calls=%fused_computation.120 | loop fusion | bytes 235008
  14.8 1.6 %multiply_convert_fusion.2 = bf16[256,320]{0,1:T(8,128)(2,1)} fusion(f32[40,8,2,128]{3,2,1,0:T(2,128)S(1)} %bitcast.209, f32[320]{0:T(512)} %param.18, f32[320]{0:T(512)} %param.17, f32[320]{0:T(512)S(1)} %mul.81, f32[320]{0:T(512)S(1)} %sub.57), kind=kLoop, calls=%fused_computation.67 | loop fusion | flops 737280 | bytes 496640 | tf_op jit(solution)/shard_map/convert_element_type | solution.py:104
  18.7 1.3 collective-permute-start.20
  20.7 3.9 %collective-permute-done.3 = bf16[4,9,1600]{2,0,1:T(4,128)(2,1)S(1)} collective-permute-done((bf16[4,9,1600]{2,0,1:T(4,128)(2,1)S(1)}, bf16[4,9,1600]{2,0,1:T(4,128)(2,1)S(1)}, u32[]{:S(2)}, u32[]{:S(2)}) %collective-permute-start.3) | collective-permute-done | bytes 115232 | tf_op jit(solution)/shard_map/ppermute | solution.py:61
  26.7 5.0 %collective-permute-done.4 = bf16[4,9,1600]{2,0,1:T(4,128)(2,1)S(1)} collective-permute-done((bf16[4,9,1600]{2,0,1:T(4,128)(2,1)S(1)}, bf16[4,9,1600]{2,0,1:T(4,128)(2,1)S(1)}, u32[]{:S(2)}, u32[]{:S(2)}) %collective-permute-start.4) | collective-permute-done | bytes 115232 | tf_op jit(solution)/shard_map/ppermute | solution.py:61
  33.6 5.0 %collective-permute-done.5 = bf16[4,9,1600]{2,0,1:T(4,128)(2,1)S(1)} collective-permute-done((bf16[4,9,1600]{2,0,1:T(4,128)(2,1)S(1)}, bf16[4,9,1600]{2,0,1:T(4,128)(2,1)S(1)}, u32[]{:S(2)}, u32[]{:S(2)}) %collective-permute-start.5) | collective-permute-done | bytes 115232 | tf_op jit(solution)/shard_map/ppermute | solution.py:61
  40.6 5.0 %collective-permute-done.6 = bf16[4,9,1600]{2,0,1:T(4,128)(2,1)S(1)} collective-permute-done((bf16[4,9,1600]{2,0,1:T(4,128)(2,1)S(1)}, bf16[4,9,1600]{2,0,1:T(4,128)(2,1)S(1)}, u32[]{:S(2)}, u32[]{:S(2)}) %collective-permute-start.6) | collective-permute-done | bytes 115232 | tf_op jit(solution)/shard_map/ppermute | solution.py:61
  47.6 5.0 %collective-permute-done.7 = bf16[4,9,1600]{2,0,1:T(4,128)(2,1)S(1)} collective-permute-done((bf16[4,9,1600]{2,0,1:T(4,128)(2,1)S(1)}, bf16[4,9,1600]{2,0,1:T(4,128)(2,1)S(1)}, u32[]{:S(2)}, u32[]{:S(2)}) %collective-permute-start.7) | collective-permute-done | bytes 115232 | tf_op jit(solution)/shard_map/ppermute | solution.py:61
  54.5 5.0 %collective-permute-done.8 = bf16[4,9,1600]{2,0,1:T(4,128)(2,1)S(1)} collective-permute-done((bf16[4,9,1600]{2,0,1:T(4,128)(2,1)S(1)}, bf16[4,9,1600]{2,0,1:T(4,128)(2,1)S(1)}, u32[]{:S(2)}, u32[]{:S(2)}) %collective-permute-start.8) | collective-permute-done | bytes 115232 | tf_op jit(solution)/shard_map/ppermute | solution.py:61
  61.5 5.0 %collective-permute-done.9 = bf16[4,9,1600]{2,0,1:T(4,128)(2,1)S(1)} collective-permute-done((bf16[4,9,1600]{2,0,1:T(4,128)(2,1)S(1)}, bf16[4,9,1600]{2,0,1:T(4,128)(2,1)S(1)}, u32[]{:S(2)}, u32[]{:S(2)}) %collective-permute-start.9) | collective-permute-done | bytes 115232 | tf_op jit(solution)/shard_map/ppermute | solution.py:61
  68.5 5.0 %collective-permute-done.10 = bf16[4,9,1600]{2,0,1:T(4,128)(2,1)S(1)} collective-permute-done((bf16[4,9,1600]{2,0,1:T(4,128)(2,1)S(1)}, bf16[4,9,1600]{2,0,1:T(4,128)(2,1)S(1)}, u32[]{:S(2)}, u32[]{:S(2)}) %collective-permute-start.10) | collective-permute-done | bytes 115232 | tf_op jit(solution)/shard_map/ppermute | solution.py:61
  75.5 5.0 %collective-permute-done.11 = bf16[4,9,1600]{2,0,1:T(4,128)(2,1)S(1)} collective-permute-done((bf16[4,9,1600]{2,0,1:T(4,128)(2,1)S(1)}, bf16[4,9,1600]{2,0,1:T(4,128)(2,1)S(1)}, u32[]{:S(2)}, u32[]{:S(2)}) %collective-permute-start.11) | collective-permute-done | bytes 115232 | tf_op jit(solution)/shard_map/ppermute | solution.py:61
  82.4 5.0 %collective-permute-done.12 = bf16[4,9,1600]{2,0,1:T(4,128)(2,1)S(1)} collective-permute-done((bf16[4,9,1600]{2,0,1:T(4,128)(2,1)S(1)}, bf16[4,9,1600]{2,0,1:T(4,128)(2,1)S(1)}, u32[]{:S(2)}, u32[]{:S(2)}) %collective-permute-start.12) | collective-permute-done | bytes 115232 | tf_op jit(solution)/shard_map/ppermute | solution.py:61
  89.4 5.0 %collective-permute-done.13 = bf16[4,9,1600]{2,0,1:T(4,128)(2,1)S(1)} collective-permute-done((bf16[4,9,1600]{2,0,1:T(4,128)(2,1)S(1)}, bf16[4,9,1600]{2,0,1:T(4,128)(2,1)S(1)}, u32[]{:S(2)}, u32[]{:S(2)}) %collective-permute-start.13) | collective-permute-done | bytes 115232 | tf_op jit(solution)/shard_map/ppermute | solution.py:61
  96.4 5.0 %collective-permute-done.14 = bf16[4,9,1600]{2,0,1:T(4,128)(2,1)S(1)} collective-permute-done((bf16[4,9,1600]{2,0,1:T(4,128)(2,1)S(1)}, bf16[4,9,1600]{2,0,1:T(4,128)(2,1)S(1)}, u32[]{:S(2)}, u32[]{:S(2)}) %collective-permute-start.14) | collective-permute-done | bytes 115232 | tf_op jit(solution)/shard_map/ppermute | solution.py:61
  103.3 5.0 %collective-permute-done.15 = bf16[4,9,1600]{2,0,1:T(4,128)(2,1)S(1)} collective-permute-done((bf16[4,9,1600]{2,0,1:T(4,128)(2,1)S(1)}, bf16[4,9,1600]{2,0,1:T(4,128)(2,1)S(1)}, u32[]{:S(2)}, u32[]{:S(2)}) %collective-permute-start.15) | collective-permute-done | bytes 115232 | tf_op jit(solution)/shard_map/ppermute | solution.py:61
  109.7 1.6 %bitcast_dynamic-update-slice_fusion.1 = bf16[16,4,9,1600]{3,1,2,0:T(4,128)(2,1)} fusion(bf16[16,4,9,1600]{3,1,2,0:T(4,128)(2,1)} %bitcast_dynamic-update-slice_fusion.2, bf16[4,9,1600]{2,0,1:T(4,128)(2,1)} %collective-permute-done.32), kind=kLoop, calls=%fused_computation.106 | loop fusion | bytes 239616
  111.3 4.0 %collective-permute-done.16 = bf16[4,9,1600]{2,0,1:T(4,128)(2,1)S(1)} collective-permute-done((bf16[4,9,1600]{2,0,1:T(4,128)(2,1)S(1)}, bf16[4,9,1600]{2,0,1:T(4,128)(2,1)S(1)}, u32[]{:S(2)}, u32[]{:S(2)}) %collective-permute-start.16) | collective-permute-done | bytes 115232 | tf_op jit(solution)/shard_map/ppermute | solution.py:61
  116.0 3.8 %gather_fusion = bf16[16,4,9,1600]{3,1,2,0:T(4,128)(2,1)S(1)} fusion(bf16[16,4,9,1600]{3,1,2,0:T(4,128)(2,1)} %bitcast_dynamic-update-slice_fusion.16, s32[1024]{0:T(1024)S(1)} %pad_clamp_fusion), kind=kCustom, calls=%fused_computation | custom fusion | bytes 3686464 | tf_op jit(solution)/shard_map/gather | solution.py:63
  119.8 1.5 copy.25
  121.3 4.2 %reshape_reshape.6 = bf16[4,9,80,320]{3,2,1,0:T(8,128)(2,1)S(1)} reshape(bf16[4,9,16,1600]{3,2,1,0:T(8,128)(2,1)} %copy.25) | data formatting | bytes 3686400 | tf_op jit(solution)/shard_map/reshape;reshape | solution.py:52
  128.2 4.3 %collective-permute-start.17 = (bf16[1,128,320]{1,2,0:T(8,128)(2,1)S(1)}, bf16[1,128,320]{1,2,0:T(8,128)(2,1)S(1)}, u32[]{:S(2)}, u32[]{:S(2)}) collective-permute-start(bf16[1,128,320]{1,2,0:T(8,128)(2,1)S(1)} %get-tuple-element.25), channel_id=1, source_target_pairs={{0,1},{2,3},{4,5},{6,7},{8,9},{10,11},{12,13},{14,15},{16,17},{18,... | collective-permute-start | bytes 245768 | tf_op jit(solution)/shard_map/ppermute | solution.py:20
  132.4 1.5 %collective-permute-start.18 = (bf16[1,128,320]{1,2,0:T(8,128)(2,1)S(1)}, bf16[1,128,320]{1,2,0:T(8,128)(2,1)S(1)}, u32[]{:S(2)}, u32[]{:S(2)}) collective-permute-start(bf16[1,128,320]{1,2,0:T(8,128)(2,1)S(1)} %get-tuple-element.26), channel_id=1, source_target_pairs={{1,0},{3,2},{5,4},{7,6},{9,8},{11,10},{13,12},{15,14},{17,16},{19,... | collective-permute-start | bytes 245768 | tf_op jit(solution)/shard_map/ppermute | solution.py:21
  134.0 1.6 %bitcast_dynamic-update-slice_fusion = bf16[16,4,9,1600]{3,1,2,0:T(4,128)(2,1)} fusion(bf16[16,4,9,1600]{3,1,2,0:T(4,128)(2,1)} %bitcast_dynamic-update-slice_fusion.1, bf16[4,9,1600]{2,0,1:T(4,128)(2,1)} %collective-permute-done.33), kind=kLoop, calls=%fused_computation.105 | loop fusion | bytes 239616 | tf_op jit(solution)/shard_map/stack | solution.py:63
  135.6 3.8 %gather_fusion.1 = bf16[16,4,9,1600]{3,1,2,0:T(4,128)(2,1)S(1)} fusion(bf16[16,4,9,1600]{3,1,2,0:T(4,128)(2,1)} %bitcast_dynamic-update-slice_fusion, s32[1024]{0:T(1024)S(1)} %pad_clamp_fusion), kind=kCustom, calls=%fused_computation.1 | custom fusion | bytes 3686464 | tf_op jit(solution)/shard_map/gather | solution.py:63
  139.4 1.5 %copy.39 = bf16[4,9,16,1600]{3,2,1,0:T(8,128)(2,1)} copy(bf16[4,9,16,1600]{3,0,1,2:T(4,128)(2,1)S(1)} %bitcast.205) | data formatting | bytes 3686400 | tf_op jit(solution)/shard_map/transpose | solution.py:8
  140.9 4.2 %reshape_reshape.7 = bf16[4,9,80,320]{3,2,1,0:T(8,128)(2,1)S(1)} reshape(bf16[4,9,16,1600]{3,2,1,0:T(8,128)(2,1)} %copy.39) | data formatting | bytes 3686400 | tf_op jit(solution)/shard_map/reshape;reshape | solution.py:52
  (143 shorter events, 38.4 us)
Async XLA Ops:
  0.0 17.6 %collective-permute-start.2 = (bf16[4,9,1600]{2,0,1:T(4,128)(2,1)}, bf16[4,9,1600]{2,0,1:T(4,128)(2,1)S(1)}, u32[]{:S(2)}, u32[]{:S(2)}) collective-permute-start(bf16[4,9,1600]{2,0,1:T(4,128)(2,1)} %param.19), channel_id=1, source_target_pairs={{0,2},{2,4},{4,6},{6,8},{8,10},{10,12},{12,14},{14,16},{16,18},{18... | collective-permute-start | bytes 345608 | tf_op jit(solution)/shard_map/ppermute | solution.py:61
  3.4 13.4 %collective-permute-start = (bf16[1,128,320]{1,2,0:T(8,128)(2,1)S(1)}, bf16[1,128,320]{1,2,0:T(8,128)(2,1)S(1)}, u32[]{:S(2)}, u32[]{:S(2)}) collective-permute-start(bf16[1,128,320]{1,2,0:T(8,128)(2,1)S(1)} %get-tuple-element.29), channel_id=1, source_target_pairs={{0,1},{2,3},{4,5},{6,7},{8,9},{10,11},{12,13},{14,15},{16,17},{18,... | collective-permute-start | bytes 245768 | tf_op jit(solution)/shard_map/ppermute | solution.py:20
  7.9 9.0 %collective-permute-start.1 = (bf16[1,128,320]{1,2,0:T(8,128)(2,1)S(1)}, bf16[1,128,320]{1,2,0:T(8,128)(2,1)S(1)}, u32[]{:S(2)}, u32[]{:S(2)}) collective-permute-start(bf16[1,128,320]{1,2,0:T(8,128)(2,1)S(1)} %get-tuple-element.30), channel_id=1, source_target_pairs={{1,0},{3,2},{5,4},{7,6},{9,8},{11,10},{13,12},{15,14},{17,16},{19,... | collective-permute-start | bytes 245768 | tf_op jit(solution)/shard_map/ppermute | solution.py:21
  9.2 9.6 %collective-permute-start.19 = (bf16[4,9,1600]{2,0,1:T(4,128)(2,1)}, bf16[4,9,1600]{2,0,1:T(4,128)(2,1)S(1)}, u32[]{:S(2)}, u32[]{:S(2)}) collective-permute-start(bf16[4,9,1600]{2,0,1:T(4,128)(2,1)} %param.26), channel_id=1, source_target_pairs={{0,2},{2,4},{4,6},{6,8},{8,10},{10,12},{12,14},{14,16},{16,18},{18... | collective-permute-start | bytes 345608 | tf_op jit(solution)/shard_map/ppermute | solution.py:61
  17.7 7.0 %collective-permute-start.3 = (bf16[4,9,1600]{2,0,1:T(4,128)(2,1)S(1)}, bf16[4,9,1600]{2,0,1:T(4,128)(2,1)S(1)}, u32[]{:S(2)}, u32[]{:S(2)}) collective-permute-start(bf16[4,9,1600]{2,0,1:T(4,128)(2,1)S(1)} %collective-permute-done.2), channel_id=1, source_target_pairs={{0,2},{2,4},{4,6},{6,8},{8,10},{10,12},{12,14},{14,16},{16,18},{18... | collective-permute-start | bytes 345608 | tf_op jit(solution)/shard_map/ppermute | solution.py:61
  18.7 7.3 %collective-permute-start.20 = (bf16[4,9,1600]{2,0,1:T(4,128)(2,1)S(1)}, bf16[4,9,1600]{2,0,1:T(4,128)(2,1)S(1)}, u32[]{:S(2)}, u32[]{:S(2)}) collective-permute-start(bf16[4,9,1600]{2,0,1:T(4,128)(2,1)S(1)} %collective-permute-done.19), channel_id=1, source_target_pairs={{0,2},{2,4},{4,6},{6,8},{8,10},{10,12},{12,14},{14,16},{16,18},{18... | collective-permute-start | bytes 345608 | tf_op jit(solution)/shard_map/ppermute | solution.py:61
  24.7 7.0 %collective-permute-start.4 = (bf16[4,9,1600]{2,0,1:T(4,128)(2,1)S(1)}, bf16[4,9,1600]{2,0,1:T(4,128)(2,1)S(1)}, u32[]{:S(2)}, u32[]{:S(2)}) collective-permute-start(bf16[4,9,1600]{2,0,1:T(4,128)(2,1)S(1)} %collective-permute-done.3), channel_id=1, source_target_pairs={{0,2},{2,4},{4,6},{6,8},{8,10},{10,12},{12,14},{14,16},{16,18},{18... | collective-permute-start | bytes 345608 | tf_op jit(solution)/shard_map/ppermute | solution.py:61
  26.0 7.0 %collective-permute-start.21 = (bf16[4,9,1600]{2,0,1:T(4,128)(2,1)S(1)}, bf16[4,9,1600]{2,0,1:T(4,128)(2,1)S(1)}, u32[]{:S(2)}, u32[]{:S(2)}) collective-permute-start(bf16[4,9,1600]{2,0,1:T(4,128)(2,1)S(1)} %collective-permute-done.20), channel_id=1, source_target_pairs={{0,2},{2,4},{4,6},{6,8},{8,10},{10,12},{12,14},{14,16},{16,18},{18... | collective-permute-start | bytes 345608 | tf_op jit(solution)/shard_map/ppermute | solution.py:61
  31.7 7.0 %collective-permute-start.5 = (bf16[4,9,1600]{2,0,1:T(4,128)(2,1)S(1)}, bf16[4,9,1600]{2,0,1:T(4,128)(2,1)S(1)}, u32[]{:S(2)}, u32[]{:S(2)}) collective-permute-start(bf16[4,9,1600]{2,0,1:T(4,128)(2,1)S(1)} %collective-permute-done.4), channel_id=1, source_target_pairs={{0,2},{2,4},{4,6},{6,8},{8,10},{10,12},{12,14},{14,16},{16,18},{18... | collective-permute-start | bytes 345608 | tf_op jit(solution)/shard_map/ppermute | solution.py:61
  32.9 7.0 %collective-permute-start.22 = (bf16[4,9,1600]{2,0,1:T(4,128)(2,1)S(1)}, bf16[4,9,1600]{2,0,1:T(4,128)(2,1)S(1)}, u32[]{:S(2)}, u32[]{:S(2)}) collective-permute-start(bf16[4,9,1600]{2,0,1:T(4,128)(2,1)S(1)} %collective-permute-done.21), channel_id=1, source_target_pairs={{0,2},{2,4},{4,6},{6,8},{8,10},{10,12},{12,14},{14,16},{16,18},{18... | collective-permute-start | bytes 345608 | tf_op jit(solution)/shard_map/ppermute | solution.py:61
  38.6 7.0 %collective-permute-start.6 = (bf16[4,9,1600]{2,0,1:T(4,128)(2,1)S(1)}, bf16[4,9,1600]{2,0,1:T(4,128)(2,1)S(1)}, u32[]{:S(2)}, u32[]{:S(2)}) collective-permute-start(bf16[4,9,1600]{2,0,1:T(4,128)(2,1)S(1)} %collective-permute-done.5), channel_id=1, source_target_pairs={{0,2},{2,4},{4,6},{6,8},{8,10},{10,12},{12,14},{14,16},{16,18},{18... | collective-permute-start | bytes 345608 | tf_op jit(solution)/shard_map/ppermute | solution.py:61
  39.9 7.0 %collective-permute-start.23 = (bf16[4,9,1600]{2,0,1:T(4,128)(2,1)S(1)}, bf16[4,9,1600]{2,0,1:T(4,128)(2,1)S(1)}, u32[]{:S(2)}, u32[]{:S(2)}) collective-permute-start(bf16[4,9,1600]{2,0,1:T(4,128)(2,1)S(1)} %collective-permute-done.22), channel_id=1, source_target_pairs={{0,2},{2,4},{4,6},{6,8},{8,10},{10,12},{12,14},{14,16},{16,18},{18... | collective-permute-start | bytes 345608 | tf_op jit(solution)/shard_map/ppermute | solution.py:61
  45.6 7.0 %collective-permute-start.7 = (bf16[4,9,1600]{2,0,1:T(4,128)(2,1)S(1)}, bf16[4,9,1600]{2,0,1:T(4,128)(2,1)S(1)}, u32[]{:S(2)}, u32[]{:S(2)}) collective-permute-start(bf16[4,9,1600]{2,0,1:T(4,128)(2,1)S(1)} %collective-permute-done.6), channel_id=1, source_target_pairs={{0,2},{2,4},{4,6},{6,8},{8,10},{10,12},{12,14},{14,16},{16,18},{18... | collective-permute-start | bytes 345608 | tf_op jit(solution)/shard_map/ppermute | solution.py:61
  46.9 7.0 %collective-permute-start.24 = (bf16[4,9,1600]{2,0,1:T(4,128)(2,1)S(1)}, bf16[4,9,1600]{2,0,1:T(4,128)(2,1)S(1)}, u32[]{:S(2)}, u32[]{:S(2)}) collective-permute-start(bf16[4,9,1600]{2,0,1:T(4,128)(2,1)S(1)} %collective-permute-done.23), channel_id=1, source_target_pairs={{0,2},{2,4},{4,6},{6,8},{8,10},{10,12},{12,14},{14,16},{16,18},{18... | collective-permute-start | bytes 345608 | tf_op jit(solution)/shard_map/ppermute | solution.py:61
  52.6 7.0 %collective-permute-start.8 = (bf16[4,9,1600]{2,0,1:T(4,128)(2,1)S(1)}, bf16[4,9,1600]{2,0,1:T(4,128)(2,1)S(1)}, u32[]{:S(2)}, u32[]{:S(2)}) collective-permute-start(bf16[4,9,1600]{2,0,1:T(4,128)(2,1)S(1)} %collective-permute-done.7), channel_id=1, source_target_pairs={{0,2},{2,4},{4,6},{6,8},{8,10},{10,12},{12,14},{14,16},{16,18},{18... | collective-permute-start | bytes 345608 | tf_op jit(solution)/shard_map/ppermute | solution.py:61
  53.9 7.0 %collective-permute-start.25 = (bf16[4,9,1600]{2,0,1:T(4,128)(2,1)S(1)}, bf16[4,9,1600]{2,0,1:T(4,128)(2,1)S(1)}, u32[]{:S(2)}, u32[]{:S(2)}) collective-permute-start(bf16[4,9,1600]{2,0,1:T(4,128)(2,1)S(1)} %collective-permute-done.24), channel_id=1, source_target_pairs={{0,2},{2,4},{4,6},{6,8},{8,10},{10,12},{12,14},{14,16},{16,18},{18... | collective-permute-start | bytes 345608 | tf_op jit(solution)/shard_map/ppermute | solution.py:61
  59.5 7.0 %collective-permute-start.9 = (bf16[4,9,1600]{2,0,1:T(4,128)(2,1)S(1)}, bf16[4,9,1600]{2,0,1:T(4,128)(2,1)S(1)}, u32[]{:S(2)}, u32[]{:S(2)}) collective-permute-start(bf16[4,9,1600]{2,0,1:T(4,128)(2,1)S(1)} %collective-permute-done.8), channel_id=1, source_target_pairs={{0,2},{2,4},{4,6},{6,8},{8,10},{10,12},{12,14},{14,16},{16,18},{18... | collective-permute-start | bytes 345608 | tf_op jit(solution)/shard_map/ppermute | solution.py:61
  60.8 7.0 %collective-permute-start.26 = (bf16[4,9,1600]{2,0,1:T(4,128)(2,1)S(1)}, bf16[4,9,1600]{2,0,1:T(4,128)(2,1)S(1)}, u32[]{:S(2)}, u32[]{:S(2)}) collective-permute-start(bf16[4,9,1600]{2,0,1:T(4,128)(2,1)S(1)} %collective-permute-done.25), channel_id=1, source_target_pairs={{0,2},{2,4},{4,6},{6,8},{8,10},{10,12},{12,14},{14,16},{16,18},{18... | collective-permute-start | bytes 345608 | tf_op jit(solution)/shard_map/ppermute | solution.py:61
  66.5 7.0 %collective-permute-start.10 = (bf16[4,9,1600]{2,0,1:T(4,128)(2,1)S(1)}, bf16[4,9,1600]{2,0,1:T(4,128)(2,1)S(1)}, u32[]{:S(2)}, u32[]{:S(2)}) collective-permute-start(bf16[4,9,1600]{2,0,1:T(4,128)(2,1)S(1)} %collective-permute-done.9), channel_id=1, source_target_pairs={{0,2},{2,4},{4,6},{6,8},{8,10},{10,12},{12,14},{14,16},{16,18},{18... | collective-permute-start | bytes 345608 | tf_op jit(solution)/shard_map/ppermute | solution.py:61
  67.8 7.0 %collective-permute-start.27 = (bf16[4,9,1600]{2,0,1:T(4,128)(2,1)S(1)}, bf16[4,9,1600]{2,0,1:T(4,128)(2,1)S(1)}, u32[]{:S(2)}, u32[]{:S(2)}) collective-permute-start(bf16[4,9,1600]{2,0,1:T(4,128)(2,1)S(1)} %collective-permute-done.26), channel_id=1, source_target_pairs={{0,2},{2,4},{4,6},{6,8},{8,10},{10,12},{12,14},{14,16},{16,18},{18... | collective-permute-start | bytes 345608 | tf_op jit(solution)/shard_map/ppermute | solution.py:61
  73.5 7.0 %collective-permute-start.11 = (bf16[4,9,1600]{2,0,1:T(4,128)(2,1)S(1)}, bf16[4,9,1600]{2,0,1:T(4,128)(2,1)S(1)}, u32[]{:S(2)}, u32[]{:S(2)}) collective-permute-start(bf16[4,9,1600]{2,0,1:T(4,128)(2,1)S(1)} %collective-permute-done.10), channel_id=1, source_target_pairs={{0,2},{2,4},{4,6},{6,8},{8,10},{10,12},{12,14},{14,16},{16,18},{18... | collective-permute-start | bytes 345608 | tf_op jit(solution)/shard_map/ppermute | solution.py:61
  74.8 7.0 %collective-permute-start.28 = (bf16[4,9,1600]{2,0,1:T(4,128)(2,1)S(1)}, bf16[4,9,1600]{2,0,1:T(4,128)(2,1)S(1)}, u32[]{:S(2)}, u32[]{:S(2)}) collective-permute-start(bf16[4,9,1600]{2,0,1:T(4,128)(2,1)S(1)} %collective-permute-done.27), channel_id=1, source_target_pairs={{0,2},{2,4},{4,6},{6,8},{8,10},{10,12},{12,14},{14,16},{16,18},{18... | collective-permute-start | bytes 345608 | tf_op jit(solution)/shard_map/ppermute | solution.py:61
  80.4 7.0 %collective-permute-start.12 = (bf16[4,9,1600]{2,0,1:T(4,128)(2,1)S(1)}, bf16[4,9,1600]{2,0,1:T(4,128)(2,1)S(1)}, u32[]{:S(2)}, u32[]{:S(2)}) collective-permute-start(bf16[4,9,1600]{2,0,1:T(4,128)(2,1)S(1)} %collective-permute-done.11), channel_id=1, source_target_pairs={{0,2},{2,4},{4,6},{6,8},{8,10},{10,12},{12,14},{14,16},{16,18},{18... | collective-permute-start | bytes 345608 | tf_op jit(solution)/shard_map/ppermute | solution.py:61
  81.7 7.0 %collective-permute-start.29 = (bf16[4,9,1600]{2,0,1:T(4,128)(2,1)S(1)}, bf16[4,9,1600]{2,0,1:T(4,128)(2,1)S(1)}, u32[]{:S(2)}, u32[]{:S(2)}) collective-permute-start(bf16[4,9,1600]{2,0,1:T(4,128)(2,1)S(1)} %collective-permute-done.28), channel_id=1, source_target_pairs={{0,2},{2,4},{4,6},{6,8},{8,10},{10,12},{12,14},{14,16},{16,18},{18... | collective-permute-start | bytes 345608 | tf_op jit(solution)/shard_map/ppermute | solution.py:61
  87.4 7.0 %collective-permute-start.13 = (bf16[4,9,1600]{2,0,1:T(4,128)(2,1)S(1)}, bf16[4,9,1600]{2,0,1:T(4,128)(2,1)S(1)}, u32[]{:S(2)}, u32[]{:S(2)}) collective-permute-start(bf16[4,9,1600]{2,0,1:T(4,128)(2,1)S(1)} %collective-permute-done.12), channel_id=1, source_target_pairs={{0,2},{2,4},{4,6},{6,8},{8,10},{10,12},{12,14},{14,16},{16,18},{18... | collective-permute-start | bytes 345608 | tf_op jit(solution)/shard_map/ppermute | solution.py:61
  88.7 7.0 %collective-permute-start.30 = (bf16[4,9,1600]{2,0,1:T(4,128)(2,1)S(1)}, bf16[4,9,1600]{2,0,1:T(4,128)(2,1)S(1)}, u32[]{:S(2)}, u32[]{:S(2)}) collective-permute-start(bf16[4,9,1600]{2,0,1:T(4,128)(2,1)S(1)} %collective-permute-done.29), channel_id=1, source_target_pairs={{0,2},{2,4},{4,6},{6,8},{8,10},{10,12},{12,14},{14,16},{16,18},{18... | collective-permute-start | bytes 345608 | tf_op jit(solution)/shard_map/ppermute | solution.py:61
  94.4 7.0 %collective-permute-start.14 = (bf16[4,9,1600]{2,0,1:T(4,128)(2,1)S(1)}, bf16[4,9,1600]{2,0,1:T(4,128)(2,1)S(1)}, u32[]{:S(2)}, u32[]{:S(2)}) collective-permute-start(bf16[4,9,1600]{2,0,1:T(4,128)(2,1)S(1)} %collective-permute-done.13), channel_id=1, source_target_pairs={{0,2},{2,4},{4,6},{6,8},{8,10},{10,12},{12,14},{14,16},{16,18},{18... | collective-permute-start | bytes 345608 | tf_op jit(solution)/shard_map/ppermute | solution.py:61
  95.7 7.0 %collective-permute-start.31 = (bf16[4,9,1600]{2,0,1:T(4,128)(2,1)S(1)}, bf16[4,9,1600]{2,0,1:T(4,128)(2,1)S(1)}, u32[]{:S(2)}, u32[]{:S(2)}) collective-permute-start(bf16[4,9,1600]{2,0,1:T(4,128)(2,1)S(1)} %collective-permute-done.30), channel_id=1, source_target_pairs={{0,2},{2,4},{4,6},{6,8},{8,10},{10,12},{12,14},{14,16},{16,18},{18... | collective-permute-start | bytes 345608 | tf_op jit(solution)/shard_map/ppermute | solution.py:61
  102.6 7.1 %collective-permute-start.32 = (bf16[4,9,1600]{2,0,1:T(4,128)(2,1)S(1)}, bf16[4,9,1600]{2,0,1:T(4,128)(2,1)}, u32[]{:S(2)}, u32[]{:S(2)}) collective-permute-start(bf16[4,9,1600]{2,0,1:T(4,128)(2,1)S(1)} %collective-permute-done.31), channel_id=1, source_target_pairs={{0,2},{2,4},{4,6},{6,8},{8,10},{10,12},{12,14},{14,16},{16,18},{18... | collective-permute-start | bytes 345608 | tf_op jit(solution)/shard_map/ppermute | solution.py:61
  109.7 24.3 %collective-permute-start.33 = (bf16[4,9,1600]{2,0,1:T(4,128)(2,1)}, bf16[4,9,1600]{2,0,1:T(4,128)(2,1)}, u32[]{:S(2)}, u32[]{:S(2)}) collective-permute-start(bf16[4,9,1600]{2,0,1:T(4,128)(2,1)} %collective-permute-done.32), channel_id=1, source_target_pairs={{0,2},{2,4},{4,6},{6,8},{8,10},{10,12},{12,14},{14,16},{16,18},{18... | collective-permute-start | bytes 345608 | tf_op jit(solution)/shard_map/ppermute | solution.py:61
  128.2 17.4 %collective-permute-start.17 = (bf16[1,128,320]{1,2,0:T(8,128)(2,1)S(1)}, bf16[1,128,320]{1,2,0:T(8,128)(2,1)S(1)}, u32[]{:S(2)}, u32[]{:S(2)}) collective-permute-start(bf16[1,128,320]{1,2,0:T(8,128)(2,1)S(1)} %get-tuple-element.25), channel_id=1, source_target_pairs={{0,1},{2,3},{4,5},{6,7},{8,9},{10,11},{12,13},{14,15},{16,17},{18,... | collective-permute-start | bytes 245768 | tf_op jit(solution)/shard_map/ppermute | solution.py:20
  132.4 13.1 %collective-permute-start.18 = (bf16[1,128,320]{1,2,0:T(8,128)(2,1)S(1)}, bf16[1,128,320]{1,2,0:T(8,128)(2,1)S(1)}, u32[]{:S(2)}, u32[]{:S(2)}) collective-permute-start(bf16[1,128,320]{1,2,0:T(8,128)(2,1)S(1)} %get-tuple-element.26), channel_id=1, source_target_pairs={{1,0},{3,2},{5,4},{7,6},{9,8},{11,10},{13,12},{15,14},{17,16},{19,... | collective-permute-start | bytes 245768 | tf_op jit(solution)/shard_map/ppermute | solution.py:21
  (11 other events, 70.4 us)
